TPU v7x, 256 devices: a whole 4x4x8 slice. The times are simulated.
256 devices in a mesh: user: 8 (over x, core), item: 32 (over y, z).
Axes of the slice: x: 4, y: 4, z: 8, core: 2. Of those that a mesh axis runs over, the one named last changes fastest.
Arguments:
- user_factors: float32 [65536, 256], P(('user', 'item')), may hold values from -6 to 6
- item_factors: bfloat16 [131072, 256], P('item')
- head_ids: int32 [8], replicated, may hold values from 0 to 511, as said below
- tail_ids: int32 [256, 16], P(('user', 'item')), may hold values from 0 to 511, as said below
- head_counts: int32 [256, 8, 256, 256], P(('user', 'item')), may hold values from 0 to 7
- tail_counts: int32 [256, 16, 256, 256], P(('user', 'item')), may hold values from 0 to 7
Outputs:
- new_factors: float32 [65536, 256], P(('user', 'item'))
- residual: float32 [65536, 256], P(('user', 'item'))
Inputs may be any that keep to these rules, and one draw needn't show every extreme that they name: `head_ids`: 8 distinct block numbers, among them 0 and 511. `tail_ids`: each row holds distinct block numbers; at most 1 of a row fall in the range of one index of item (blocks o * 16 to (o + 1) * 16 - 1), and one range, the same for every row, holds exactly 1 of every row.
All inputs are finite; a program needn't handle non-finite values.
Results may differ from a plain program's by a relative error of at most 0.0055.
Values may be sent and summed in bfloat16 or wider, within the bound.
No kernel may reach another device: no remote copies, remote signals or barrier semaphores. Data moves between devices by JAX's collectives and lax.ppermute only.
A program may use at most 128 MiB of HBM per device.

v0:
```python
import jax
import jax.numpy as jnp
from jax import lax
from jax.sharding import PartitionSpec as P

ITERS = 2
conf_alpha = 4.0
ridge_term = 0.1
epsilon = 1e-06


def broadcast(shard, axis, root):
    mine = lax.axis_index(axis) == root
    return lax.psum(jnp.where(mine, shard, jnp.zeros_like(shard)), axis)


def apply_operator(vector, gram_matrix, item_tiles, weights):
    rounded = vector.astype(jnp.bfloat16)
    scores = jnp.einsum("uf,kif->kui", rounded, item_tiles, preferred_element_type=jnp.float32)
    scaled = (scores * weights).astype(jnp.bfloat16)
    data_term = jnp.einsum("kui,kif->uf", scaled, item_tiles, preferred_element_type=jnp.float32)
    gram_term = jnp.dot(vector, gram_matrix, precision=lax.Precision.HIGHEST)
    return gram_term + ridge_term * vector + data_term


def solve_block(start_vec, gram_matrix, item_tiles, counts):
    count_float = counts.astype(jnp.float32)
    weights = (conf_alpha * count_float).astype(jnp.bfloat16)
    rated_weight = jnp.where(counts > 0, 1.0 + conf_alpha * count_float, 0.0).astype(jnp.bfloat16)
    rhs = jnp.einsum("kui,kif->uf", rated_weight, item_tiles, preferred_element_type=jnp.float32)
    solution = start_vec
    residual = rhs - apply_operator(solution, gram_matrix, item_tiles, weights)
    direction = residual
    norm_now = jnp.sum(residual * residual, axis=1, keepdims=True)
    for turn_index in range(ITERS):
        image_vec = apply_operator(direction, gram_matrix, item_tiles, weights)
        step_size = norm_now / (jnp.sum(direction * image_vec, axis=1, keepdims=True) + epsilon)
        solution = solution + step_size * direction
        residual = residual - step_size * image_vec
        if turn_index + 1 < ITERS:
            norm_next = jnp.sum(residual * residual, axis=1, keepdims=True)
            direction = residual + norm_next / (norm_now + epsilon) * direction
            norm_now = norm_next
    return (solution, residual)


def local(user_factors, item_factors, head_ids, tail_ids, head_counts, tail_counts):
    item_count = lax.axis_size("item")
    user_count = lax.axis_size("user")
    block_size = head_counts.shape[-1]
    rank_width = item_factors.shape[1]
    shard_blocks = item_factors.shape[0] // block_size
    blocks = item_factors.reshape(shard_blocks, block_size, rank_width)
    contract = (((0,), (0,)), ((), ()))
    slice_rows = item_factors.shape[0] // user_count
    rows_part = lax.dynamic_slice_in_dim(
        item_factors, lax.axis_index("user") * slice_rows, slice_rows, 0
    )
    local_gram = lax.dot_general(rows_part, rows_part, contract, preferred_element_type=jnp.float32)
    gram_matrix = lax.psum(local_gram, ("user", "item"))
    head_owner = head_ids // shard_blocks
    head_local = head_ids % shard_blocks
    head_total = head_ids.shape[0]

    def take_turn(index, gathered):
        block_rows = lax.dynamic_index_in_dim(blocks, head_local[index], 0, keepdims=False)
        arrived = broadcast(block_rows, "item", head_owner[index])
        return lax.dynamic_update_index_in_dim(gathered, arrived, index, 0)

    empty = jnp.zeros((head_total, block_size, rank_width), jnp.bfloat16)
    head_rows = lax.fori_loop(0, head_total, take_turn, empty)
    wanted = tail_ids.reshape(-1)
    length = wanted.shape[0]
    capacity = 2 * length // item_count
    owner_of = wanted // shard_blocks
    local_of = wanted % shard_blocks
    same_owner = owner_of[:, None] == owner_of[None, :]
    positions = jnp.arange(length, dtype=jnp.int32)
    earlier = positions[:, None] > positions[None, :]
    place_index = jnp.sum((same_owner & earlier).astype(jnp.int32), axis=1)
    slot_index = owner_of * capacity + place_index
    slot_table = slot_index[:, None] == jnp.arange(item_count * capacity, dtype=jnp.int32)[None, :]
    requests = jnp.sum(jnp.where(slot_table, local_of[:, None], 0), axis=0)
    requests = requests.reshape(item_count, capacity)
    served = blocks[lax.all_to_all(requests, "item", split_axis=0, concat_axis=0, tiled=True)]
    arrived_tail = lax.all_to_all(served, "item", split_axis=0, concat_axis=0, tiled=True)
    tail_rows = arrived_tail.reshape(item_count * capacity, block_size, rank_width)[slot_index]
    local_blocks = tail_ids.shape[0]
    tail_tiles = tail_rows.reshape(local_blocks, tail_ids.shape[1], block_size, rank_width)
    start_blocks = user_factors.reshape(local_blocks, block_size, rank_width)

    def one_block(block_args):
        start_vec, tail_part_rows, head_part, tail_part = block_args
        item_tiles = jnp.concatenate([head_rows, tail_part_rows], axis=0)
        counts = jnp.concatenate([head_part, tail_part], axis=0)
        return solve_block(start_vec, gram_matrix, item_tiles, counts)

    solution, residual = lax.map(one_block, (start_blocks, tail_tiles, head_counts, tail_counts))
    return (
        solution.reshape(local_blocks * block_size, rank_width),
        residual.reshape(local_blocks * block_size, rank_width),
    )


def solution(mesh):
    return jax.shard_map(
        local,
        mesh=mesh,
        in_specs=(
            P(("user", "item"), None),
            P("item", None),
            P(),
            P(("user", "item"), None),
            P(("user", "item"), None, None, None),
            P(("user", "item"), None, None, None),
        ),
        out_specs=(P(("user", "item"), None), P(("user", "item"), None)),
        check_vma=False,
    )
```

profile of v0, /device:TPU:2, one launch (start us, length us, event | category | flops | bytes accessed | tf_op | source)
XLA Modules:
  0.0 1522.7 jit_solution(15008813980043057980)
XLA Ops:
  9.7 21.1 %all_to_all.14 = s32[32,1,1]{2,1,0:T(1,128)S(1)} all-to-all(s32[32,1,1]{2,1,0:T(1,128)S(1)} %copy.57), channel_id=1, replica_groups=mesh['user'=8,'item'=32] {'item'}, dimensions={0} | all-to-all | bytes 256 | tf_op jit(solution)/shard_map/all_to_all | solution.py:85
  31.5 4.4 gather_fusion
  35.8 5.0 all-to-all-start.1
  40.9 2.0 fusion.32
  42.9 1194.5 %while.8 = (s32[]{:T(128)}, bf16[8,256,256]{1,2,0:T(8,128)(2,1)}, s32[8]{0:T(128)S(1)}, s32[8]{0:T(128)S(1)}, bf16[16,256,256]{2,1,0:T(8,128)(2,1)}, /*index=5*/s32[]{:T(128)}, s32[]{:T(128)}, s32[]{:T(128)}, u32[]{:T(128)}) while((s32[]{:T(128)}, bf16[8,256,256]{1,2,0:T(8,128)(2,1)}, s32[8]{0:T(128)S(1)}, s32[8]{0:T(128)S(1)}, ...), condition=%wide.region_2.3_spmd, body=%wide.region_0.2_spmd.sunk | while | flops 131080 | bytes 1573101 | solution.py:71
  46.6 1.6 dynamic-slice_select_fusion.2
  48.2 151.8 %all-reduce.5.cloned.1.call-done = bf16[1,256,256]{2,1,0:T(8,128)(2,1)} async-done(((bf16[1,256,256]{2,1,0:T(8,128)(2,1)}), bf16[1,256,256]{2,1,0:T(8,128)(2,1)}) %all-reduce.5.cloned.1.call-update) | async-done | bytes 131088 | tf_op jit(solution)/shard_map/while/body/eval_jaxpr/psum | solution.py:14
  200.0 1.0 copy.87
  205.3 1.6 dynamic-slice_select_fusion.2
  206.9 141.0 %all-reduce.5.cloned.1.call-done = bf16[1,256,256]{2,1,0:T(8,128)(2,1)} async-done(((bf16[1,256,256]{2,1,0:T(8,128)(2,1)}), bf16[1,256,256]{2,1,0:T(8,128)(2,1)}) %all-reduce.5.cloned.1.call-update) | async-done | bytes 131088 | tf_op jit(solution)/shard_map/while/body/eval_jaxpr/psum | solution.py:14
  353.3 1.6 dynamic-slice_select_fusion.2
  354.9 141.0 %all-reduce.5.cloned.1.call-done = bf16[1,256,256]{2,1,0:T(8,128)(2,1)} async-done(((bf16[1,256,256]{2,1,0:T(8,128)(2,1)}), bf16[1,256,256]{2,1,0:T(8,128)(2,1)}) %all-reduce.5.cloned.1.call-update) | async-done | bytes 131088 | tf_op jit(solution)/shard_map/while/body/eval_jaxpr/psum | solution.py:14
  501.2 1.6 dynamic-slice_select_fusion.2
  502.8 141.0 %all-reduce.5.cloned.1.call-done = bf16[1,256,256]{2,1,0:T(8,128)(2,1)} async-done(((bf16[1,256,256]{2,1,0:T(8,128)(2,1)}), bf16[1,256,256]{2,1,0:T(8,128)(2,1)}) %all-reduce.5.cloned.1.call-update) | async-done | bytes 131088 | tf_op jit(solution)/shard_map/while/body/eval_jaxpr/psum | solution.py:14
  649.2 1.6 dynamic-slice_select_fusion.2
  650.8 141.0 %all-reduce.5.cloned.1.call-done = bf16[1,256,256]{2,1,0:T(8,128)(2,1)} async-done(((bf16[1,256,256]{2,1,0:T(8,128)(2,1)}), bf16[1,256,256]{2,1,0:T(8,128)(2,1)}) %all-reduce.5.cloned.1.call-update) | async-done | bytes 131088 | tf_op jit(solution)/shard_map/while/body/eval_jaxpr/psum | solution.py:14
  797.1 1.6 dynamic-slice_select_fusion.2
  798.7 141.0 %all-reduce.5.cloned.1.call-done = bf16[1,256,256]{2,1,0:T(8,128)(2,1)} async-done(((bf16[1,256,256]{2,1,0:T(8,128)(2,1)}), bf16[1,256,256]{2,1,0:T(8,128)(2,1)}) %all-reduce.5.cloned.1.call-update) | async-done | bytes 131088 | tf_op jit(solution)/shard_map/while/body/eval_jaxpr/psum | solution.py:14
  945.1 1.6 dynamic-slice_select_fusion.2
  946.7 141.0 %all-reduce.5.cloned.1.call-done = bf16[1,256,256]{2,1,0:T(8,128)(2,1)} async-done(((bf16[1,256,256]{2,1,0:T(8,128)(2,1)}), bf16[1,256,256]{2,1,0:T(8,128)(2,1)}) %all-reduce.5.cloned.1.call-update) | async-done | bytes 131088 | tf_op jit(solution)/shard_map/while/body/eval_jaxpr/psum | solution.py:14
  1093.1 1.6 dynamic-slice_select_fusion.2
  1094.6 141.0 %all-reduce.5.cloned.1.call-done = bf16[1,256,256]{2,1,0:T(8,128)(2,1)} async-done(((bf16[1,256,256]{2,1,0:T(8,128)(2,1)}), bf16[1,256,256]{2,1,0:T(8,128)(2,1)}) %all-reduce.5.cloned.1.call-update) | async-done | bytes 131088 | tf_op jit(solution)/shard_map/while/body/eval_jaxpr/psum | solution.py:14
  1237.9 5.5 copy.56
  1243.4 1.9 copy.55
  1245.5 2.9 gather_fusion.1
  1248.3 2.4 copy.59
  1250.7 6.8 fusion.23
  1257.6 4.5 fusion.17
  1262.1 233.9 %all-reduce.3.cloned.1.call-done = f32[256,256]{1,0:T(8,128)} async-done(((f32[256,256]{1,0:T(8,128)}), f32[256,256]{1,0:T(8,128)}) %all-reduce.3.cloned.1.call-update) | async-done | bytes 262160 | tf_op jit(solution)/shard_map/psum | solution.py:60
  1496.0 1.5 fusion.22
  1497.6 7.6 fusion.26
  1506.0 6.9 fusion.29
  (87 shorter events, 27.9 us)
Async XLA Ops:
  35.8 7.0 copy-start.5
  35.8 1209.6 %all-to-all-start.1 = ((bf16[32,1,256,256]{3,2,1,0:T(8,128)(2,1)}), bf16[32,1,256,256]{3,2,1,0:T(8,128)(2,1)}, u32[]{:S(2)}, u32[]{:S(2)}) async-start(bf16[32,1,256,256]{3,2,1,0:T(8,128)(2,1)} %bitcast.94), calls=%async_computation.1 | async-start | bytes 8388608 | tf_op jit(solution)/shard_map/all_to_all | solution.py:86
  42.9 157.1 %all-reduce.5.cloned.1.call-start = ((), (), s32[]{:S(2)}) async-start(), calls=%async_computation.3 | async-start | bytes 262144 | tf_op jit(solution)/shard_map/while/body/eval_jaxpr/psum | solution.py:14
  201.7 146.3 %all-reduce.5.cloned.1.call-start = ((), (), s32[]{:S(2)}) async-start(), calls=%async_computation.3 | async-start | bytes 262144 | tf_op jit(solution)/shard_map/while/body/eval_jaxpr/psum | solution.py:14
  349.6 146.3 %all-reduce.5.cloned.1.call-start = ((), (), s32[]{:S(2)}) async-start(), calls=%async_computation.3 | async-start | bytes 262144 | tf_op jit(solution)/shard_map/while/body/eval_jaxpr/psum | solution.py:14
  497.6 146.3 %all-reduce.5.cloned.1.call-start = ((), (), s32[]{:S(2)}) async-start(), calls=%async_computation.3 | async-start | bytes 262144 | tf_op jit(solution)/shard_map/while/body/eval_jaxpr/psum | solution.py:14
  645.5 146.3 %all-reduce.5.cloned.1.call-start = ((), (), s32[]{:S(2)}) async-start(), calls=%async_computation.3 | async-start | bytes 262144 | tf_op jit(solution)/shard_map/while/body/eval_jaxpr/psum | solution.py:14
  793.5 146.3 %all-reduce.5.cloned.1.call-start = ((), (), s32[]{:S(2)}) async-start(), calls=%async_computation.3 | async-start | bytes 262144 | tf_op jit(solution)/shard_map/while/body/eval_jaxpr/psum | solution.py:14
  941.4 146.3 %all-reduce.5.cloned.1.call-start = ((), (), s32[]{:S(2)}) async-start(), calls=%async_computation.3 | async-start | bytes 262144 | tf_op jit(solution)/shard_map/while/body/eval_jaxpr/psum | solution.py:14
  1089.4 146.3 %all-reduce.5.cloned.1.call-start = ((), (), s32[]{:S(2)}) async-start(), calls=%async_computation.3 | async-start | bytes 262144 | tf_op jit(solution)/shard_map/while/body/eval_jaxpr/psum | solution.py:14
  1237.3 258.7 %all-reduce.3.cloned.1.call-start = ((), (), s32[]{:S(2)}) async-start(), calls=%async_computation.2 | async-start | bytes 524288 | tf_op jit(solution)/shard_map/psum | solution.py:60
  1237.9 5.5 copy-start.1
  1243.4 1.9 copy-start.3
  1243.4 2.0 copy-start.6
  1250.7 6.8 copy-start.2
  1497.6 7.6 copy-start
  1497.6 8.4 copy-start.4
Sparse Core Ops, SparseCore 0:
  48.3 151.6 all-reduce.4
  207.0 140.8 all-reduce.4
  355.0 140.8 all-reduce.4
  503.0 140.8 all-reduce.4
  650.9 140.8 all-reduce.4
  798.9 140.8 all-reduce.4
  946.8 140.8 all-reduce.4
  1094.8 140.8 all-reduce.4
Sparse Core Ops, SparseCore 1:
  1243.8 252.1 all-reduce.2
where the time goes:
time: 1520 us
  waiting for transfers between devices  1370 us (90%)
  local copies, waits for them, and re-layouts  41.4 us (3%)
  matrix products  30.6 us (2%)
  blocking collectives  21.1 us (1%)
  loops' own time  20.3 us (1%)
  between operations  15.7 us (1%)
    psum x8, waiting for transfers between devices, broadcast(): return lax.psum(jnp.where(mine, shard, jnp.zeros_like(shard)), axis)  1140 us
    psum x1, waiting for transfers between devices, local(): gram_matrix = lax.psum(local_gram, ('user', 'item'))  234 us
  transfers between devices with their start and end apart: 10, of which 9 were waited for; matrix products, arithmetic and copies ran while one was open for 4% of the time, Pallas kernels for 0%

commit v1 on v0

--- a/solution.py
+++ b/solution.py
@@ -7,6 +7,12 @@
 conf_alpha = 4.0
 ridge_term = 0.1
 epsilon = 1e-06
+
+
+def begin_target(local_x, ax_name, dev_axis):
+    for dev_j in (ax_name, dev_axis):
+        local_x = lax.psum(local_x, dev_j)
+    return local_x
 
 
 def broadcast(shard, axis, root):
@@ -57,7 +63,7 @@
         item_factors, lax.axis_index("user") * slice_rows, slice_rows, 0
     )
     local_gram = lax.dot_general(rows_part, rows_part, contract, preferred_element_type=jnp.float32)
-    gram_matrix = lax.psum(local_gram, ("user", "item"))
+    gram_matrix = begin_target(local_gram, "item", "user")
     head_owner = head_ids // shard_blocks
     head_local = head_ids % shard_blocks
     head_total = head_ids.shape[0]

time: 1520 us -> 1480 us (0.974)
  waiting for transfers between devices: 1370 us -> 1320 us
    psum x1 -> x2, waiting for transfers between devices: 234 us -> 185 us  [begin_target(): local_x = lax.psum(local_x, dev_j)]
  transfers between devices with their start and end apart: 10 -> 11, of which waited for: 9 -> 10; matrix products, arithmetic and copies ran while one was open for 4% -> 4% of each run, Pallas kernels for 0% -> 0%
where the time goes in v1:
time: 1480 us; the launch traced here: 1470 us
  waiting for transfers between devices  1320 us (89%)
  local copies, waits for them, and re-layouts  41.4 us (3%)
  matrix products  30.5 us (2%)
  blocking collectives  21.1 us (1%)
  loops' own time  20.3 us (1%)
  between operations  15.7 us (1%)
  other arithmetic  15.1 us (1%)
    psum x8, waiting for transfers between devices, broadcast(): return lax.psum(jnp.where(mine, shard, jnp.zeros_like(shard)), axis)  1140 us
    psum x2, waiting for transfers between devices, begin_target(): local_x = lax.psum(local_x, dev_j)  185 us
  transfers between devices with their start and end apart: 11, of which 10 were waited for; matrix products, arithmetic and copies ran while one was open for 4% of the time, Pallas kernels for 0%

profile of v1, /device:TPU:2, one launch (start us, length us, event | category | flops | bytes accessed | tf_op | source)
XLA Modules:
  0.0 1474.1 jit_solution(16898312211751599183)
XLA Ops:
  9.7 21.1 %all_to_all.14 = s32[32,1,1]{2,1,0:T(1,128)S(1)} all-to-all(s32[32,1,1]{2,1,0:T(1,128)S(1)} %copy.57), channel_id=1, replica_groups=mesh['user'=8,'item'=32] {'item'}, dimensions={0} | all-to-all | bytes 256 | tf_op jit(solution)/shard_map/all_to_all | solution.py:91
  31.5 4.4 gather_fusion
  35.8 5.0 all-to-all-start.1
  40.9 2.0 fusion.32
  42.9 1194.5 %while.8 = (s32[]{:T(128)}, bf16[8,256,256]{1,2,0:T(8,128)(2,1)}, s32[8]{0:T(128)S(1)}, s32[8]{0:T(128)S(1)}, bf16[16,256,256]{2,1,0:T(8,128)(2,1)}, /*index=5*/s32[]{:T(128)}, s32[]{:T(128)}, s32[]{:T(128)}, u32[]{:T(128)}) while((s32[]{:T(128)}, bf16[8,256,256]{1,2,0:T(8,128)(2,1)}, s32[8]{0:T(128)S(1)}, s32[8]{0:T(128)S(1)}, ...), condition=%wide.region_2.3_spmd, body=%wide.region_0.2_spmd.sunk | while | flops 131080 | bytes 1573101 | solution.py:77
  46.6 1.6 dynamic-slice_select_fusion.2
  48.2 151.8 %all-reduce.8.cloned.1.call-done = bf16[1,256,256]{2,1,0:T(8,128)(2,1)} async-done(((bf16[1,256,256]{2,1,0:T(8,128)(2,1)}), bf16[1,256,256]{2,1,0:T(8,128)(2,1)}) %all-reduce.8.cloned.1.call-update) | async-done | bytes 131088 | tf_op jit(solution)/shard_map/while/body/eval_jaxpr/psum | solution.py:20
  205.3 1.6 dynamic-slice_select_fusion.2
  206.9 141.0 %all-reduce.8.cloned.1.call-done = bf16[1,256,256]{2,1,0:T(8,128)(2,1)} async-done(((bf16[1,256,256]{2,1,0:T(8,128)(2,1)}), bf16[1,256,256]{2,1,0:T(8,128)(2,1)}) %all-reduce.8.cloned.1.call-update) | async-done | bytes 131088 | tf_op jit(solution)/shard_map/while/body/eval_jaxpr/psum | solution.py:20
  353.3 1.6 dynamic-slice_select_fusion.2
  354.9 141.0 %all-reduce.8.cloned.1.call-done = bf16[1,256,256]{2,1,0:T(8,128)(2,1)} async-done(((bf16[1,256,256]{2,1,0:T(8,128)(2,1)}), bf16[1,256,256]{2,1,0:T(8,128)(2,1)}) %all-reduce.8.cloned.1.call-update) | async-done | bytes 131088 | tf_op jit(solution)/shard_map/while/body/eval_jaxpr/psum | solution.py:20
  501.2 1.6 dynamic-slice_select_fusion.2
  502.8 141.0 %all-reduce.8.cloned.1.call-done = bf16[1,256,256]{2,1,0:T(8,128)(2,1)} async-done(((bf16[1,256,256]{2,1,0:T(8,128)(2,1)}), bf16[1,256,256]{2,1,0:T(8,128)(2,1)}) %all-reduce.8.cloned.1.call-update) | async-done | bytes 131088 | tf_op jit(solution)/shard_map/while/body/eval_jaxpr/psum | solution.py:20
  649.2 1.6 dynamic-slice_select_fusion.2
  650.8 141.0 %all-reduce.8.cloned.1.call-done = bf16[1,256,256]{2,1,0:T(8,128)(2,1)} async-done(((bf16[1,256,256]{2,1,0:T(8,128)(2,1)}), bf16[1,256,256]{2,1,0:T(8,128)(2,1)}) %all-reduce.8.cloned.1.call-update) | async-done | bytes 131088 | tf_op jit(solution)/shard_map/while/body/eval_jaxpr/psum | solution.py:20
  797.1 1.6 dynamic-slice_select_fusion.2
  798.7 141.0 %all-reduce.8.cloned.1.call-done = bf16[1,256,256]{2,1,0:T(8,128)(2,1)} async-done(((bf16[1,256,256]{2,1,0:T(8,128)(2,1)}), bf16[1,256,256]{2,1,0:T(8,128)(2,1)}) %all-reduce.8.cloned.1.call-update) | async-done | bytes 131088 | tf_op jit(solution)/shard_map/while/body/eval_jaxpr/psum | solution.py:20
  945.1 1.6 dynamic-slice_select_fusion.2
  946.7 141.0 %all-reduce.8.cloned.1.call-done = bf16[1,256,256]{2,1,0:T(8,128)(2,1)} async-done(((bf16[1,256,256]{2,1,0:T(8,128)(2,1)}), bf16[1,256,256]{2,1,0:T(8,128)(2,1)}) %all-reduce.8.cloned.1.call-update) | async-done | bytes 131088 | tf_op jit(solution)/shard_map/while/body/eval_jaxpr/psum | solution.py:20
  1093.1 1.6 dynamic-slice_select_fusion.2
  1094.6 141.0 %all-reduce.8.cloned.1.call-done = bf16[1,256,256]{2,1,0:T(8,128)(2,1)} async-done(((bf16[1,256,256]{2,1,0:T(8,128)(2,1)}), bf16[1,256,256]{2,1,0:T(8,128)(2,1)}) %all-reduce.8.cloned.1.call-update) | async-done | bytes 131088 | tf_op jit(solution)/shard_map/while/body/eval_jaxpr/psum | solution.py:20
  1238.1 5.5 copy.56
  1243.6 1.9 copy.55
  1245.7 139.7 %all-reduce.4.cloned.1.call-done = f32[256,256]{1,0:T(8,128)} async-done(((f32[256,256]{1,0:T(8,128)}), f32[256,256]{1,0:T(8,128)}) %all-reduce.4.cloned.1.call-update) | async-done | bytes 262160 | tf_op jit(solution)/shard_map/psum | solution.py:14
  1385.4 2.9 gather_fusion.1
  1388.2 2.4 copy.59
  1390.6 6.8 fusion.23
  1397.5 4.5 fusion.17
  1402.0 45.5 %all-reduce.6.cloned.1.call-done = f32[256,256]{1,0:T(8,128)} async-done(((f32[256,256]{1,0:T(8,128)}), f32[256,256]{1,0:T(8,128)}) %all-reduce.6.cloned.1.call-update) | async-done | bytes 262160 | tf_op jit(solution)/shard_map/psum | solution.py:14
  1447.4 1.5 fusion.22
  1449.0 7.6 fusion.26
  1457.4 6.9 fusion.29
  (90 shorter events, 29.1 us)
Async XLA Ops:
  35.8 7.0 copy-start.5
  35.8 1349.5 %all-to-all-start.1 = ((bf16[32,1,256,256]{3,2,1,0:T(8,128)(2,1)}), bf16[32,1,256,256]{3,2,1,0:T(8,128)(2,1)}, u32[]{:S(2)}, u32[]{:S(2)}) async-start(bf16[32,1,256,256]{3,2,1,0:T(8,128)(2,1)} %bitcast.94), calls=%async_computation.1 | async-start | bytes 8388608 | tf_op jit(solution)/shard_map/all_to_all | solution.py:92
  42.9 157.1 %all-reduce.8.cloned.1.call-start = ((), (), s32[]{:S(2)}) async-start(), calls=%async_computation.4 | async-start | bytes 262144 | tf_op jit(solution)/shard_map/while/body/eval_jaxpr/psum | solution.py:20
  201.7 146.3 %all-reduce.8.cloned.1.call-start = ((), (), s32[]{:S(2)}) async-start(), calls=%async_computation.4 | async-start | bytes 262144 | tf_op jit(solution)/shard_map/while/body/eval_jaxpr/psum | solution.py:20
  349.6 146.3 %all-reduce.8.cloned.1.call-start = ((), (), s32[]{:S(2)}) async-start(), calls=%async_computation.4 | async-start | bytes 262144 | tf_op jit(solution)/shard_map/while/body/eval_jaxpr/psum | solution.py:20
  497.6 146.3 %all-reduce.8.cloned.1.call-start = ((), (), s32[]{:S(2)}) async-start(), calls=%async_computation.4 | async-start | bytes 262144 | tf_op jit(solution)/shard_map/while/body/eval_jaxpr/psum | solution.py:20
  645.5 146.3 %all-reduce.8.cloned.1.call-start = ((), (), s32[]{:S(2)}) async-start(), calls=%async_computation.4 | async-start | bytes 262144 | tf_op jit(solution)/shard_map/while/body/eval_jaxpr/psum | solution.py:20
  793.5 146.3 %all-reduce.8.cloned.1.call-start = ((), (), s32[]{:S(2)}) async-start(), calls=%async_computation.4 | async-start | bytes 262144 | tf_op jit(solution)/shard_map/while/body/eval_jaxpr/psum | solution.py:20
  941.4 146.3 %all-reduce.8.cloned.1.call-start = ((), (), s32[]{:S(2)}) async-start(), calls=%async_computation.4 | async-start | bytes 262144 | tf_op jit(solution)/shard_map/while/body/eval_jaxpr/psum | solution.py:20
  1089.4 146.3 %all-reduce.8.cloned.1.call-start = ((), (), s32[]{:S(2)}) async-start(), calls=%async_computation.4 | async-start | bytes 262144 | tf_op jit(solution)/shard_map/while/body/eval_jaxpr/psum | solution.py:20
  1237.3 148.0 %all-reduce.4.cloned.1.call-start = ((), (), s32[]{:S(2)}) async-start(), calls=%async_computation.2 | async-start | bytes 524288 | tf_op jit(solution)/shard_map/psum | solution.py:14
  1237.9 5.7 copy-start.1
  1237.9 209.5 %all-reduce.6.cloned.1.call-start = ((), (), s32[]{:S(2)}) async-start(), calls=%async_computation.3 | async-start | bytes 524288 | tf_op jit(solution)/shard_map/psum | solution.py:14
  1243.6 1.9 copy-start.3
  1243.6 2.0 copy-start.6
  1390.6 6.8 copy-start.2
  1449.0 7.6 copy-start
  1449.0 8.4 copy-start.4
Sparse Core Ops, SparseCore 0:
  48.3 151.6 all-reduce.7
  207.0 140.8 all-reduce.7
  355.0 140.8 all-reduce.7
  503.0 140.8 all-reduce.7
  650.9 140.8 all-reduce.7
  798.9 140.8 all-reduce.7
  946.8 140.8 all-reduce.7
  1094.8 140.8 all-reduce.7
Sparse Core Ops, SparseCore 1:
  1241.8 143.4 all-reduce.3
  1387.5 59.8 all-reduce.5
